TPU v7x, 256 devices: a whole 4x4x8 slice. The times are simulated.
256 devices in a mesh: batch: 64 (over y, z, x_hi), mp: 4 (over x_lo, core).
Axes of the slice: x: 4 (x_hi: 2, x_lo: 2; x = x_hi * 2 + x_lo), y: 4, z: 8, core: 2. Of those that a mesh axis runs over, the one named last changes fastest.
Arguments:
- img_feat: bfloat16 [131072, 768], P(('batch', 'mp')), may hold values from -6 to 6
- txt_feat: bfloat16 [131072, 768], P(('batch', 'mp')), may hold values from -6 to 6
- img_proj: bfloat16 [768, 768], P('mp'), may hold values from -0.21875 to 0.21875
- txt_proj: bfloat16 [768, 768], P('mp'), may hold values from -0.21875 to 0.21875
- logit_scale: float32 [], replicated, may hold values from 2 to 3
- bias: float32 [], replicated, may hold values from -2 to 0
Outputs:
- mean_loss: float32 [], replicated
- grad_logit_scale: float32 [], replicated
- grad_bias: float32 [], replicated
- grad_img_proj: float32 [768, 768], P('mp')
- grad_txt_proj: float32 [768, 768], P('mp')
All inputs are finite; a program needn't handle non-finite values.
Results may differ from a plain program's by a relative error of at most 0.0008.
Values may be sent and summed in bfloat16 or wider, within the bound.
A program may use at most 128 MiB of HBM per device.

v0:
```python
import jax
import jax.numpy as jnp
from jax import lax
from jax.sharding import PartitionSpec as P

GROUP_BITS = 3


def from_partner(value, axis, bit):
    return lax.ppermute(value, axis, [(i, i ^ 1 << bit) for i in range(lax.axis_size(axis))])


def normalize(u):
    r = lax.rsqrt(jnp.sum(u * u, axis=1, keepdims=True) + 1e-06)
    zf = u * r
    return (zf, r, zf.astype(jnp.bfloat16))


def back(dz, zf, r):
    return (r * (dz - zf * jnp.sum(zf * dz, axis=1, keepdims=True))).astype(jnp.bfloat16)


def pair_terms(left, right, scale, bias):
    sims = jnp.einsum("rd,cd->rc", left, right, preferred_element_type=jnp.float32)
    width = right.shape[0]
    row_ids = lax.broadcasted_iota(jnp.int32, sims.shape, 0)
    col_ids = lax.broadcasted_iota(jnp.int32, sims.shape, 1)
    sign = jnp.where(row_ids == col_ids, 1.0, -1.0).astype(jnp.float32)
    logit = scale * sims + bias
    loss = jnp.sum(jax.nn.softplus(-sign * logit)) / width
    grads = -sign * jax.nn.sigmoid(-sign * logit) / width
    return (grads, loss, jnp.sum(grads), jnp.sum(grads * scale * sims))


def per_device(img_feat, txt_feat, img_proj, txt_proj, logit_scale, bias):
    rows = img_feat.shape[0]
    embed = img_proj.shape[1]
    img_cols = img_feat
    txt_cols = txt_feat
    u_img = jnp.dot(
        img_cols,
        lax.all_gather(img_proj, "mp", axis=0, tiled=True),
        preferred_element_type=jnp.float32,
    )
    u_txt = jnp.dot(
        txt_cols,
        lax.all_gather(txt_proj, "mp", axis=0, tiled=True),
        preferred_element_type=jnp.float32,
    )
    zf_img, r_img, z_img = normalize(u_img)
    zf_txt, r_txt, z_txt = normalize(u_txt)
    scale = jnp.exp(logit_scale)
    held = z_txt
    for section in range(GROUP_BITS):
        arrived = from_partner(held, "batch", section)
        held = jnp.concatenate([held, arrived], axis=0)
    grads, loss, gsum, gscale = pair_terms(z_img, held, scale, bias)
    grads_b = grads.astype(jnp.bfloat16)
    dz_img = scale * jnp.dot(grads_b, held, preferred_element_type=jnp.float32)
    partials = scale * jnp.einsum("rc,rd->cd", grads_b, z_img, preferred_element_type=jnp.float32)
    for section in reversed(range(GROUP_BITS)):
        half = partials.shape[0] // 2
        returned = from_partner(partials[half:], "batch", section)
        partials = partials[:half] + returned
    du_img = back(dz_img, zf_img, r_img)
    du_txt = back(partials, zf_txt, r_txt)
    img_cols = img_feat
    txt_cols = txt_feat
    local_rows = lax.psum_scatter(
        jnp.concatenate(
            [
                jnp.einsum("re,rd->ed", img_cols, du_img, preferred_element_type=jnp.float32),
                jnp.einsum("re,rd->ed", txt_cols, du_txt, preferred_element_type=jnp.float32),
            ],
            axis=1,
        ),
        "mp",
        scatter_dimension=0,
        tiled=True,
    )
    summed = lax.psum(local_rows, "batch")
    loss_sum, gsum_all, gscale_all = lax.psum((loss, gsum, gscale), ("batch", "mp"))
    images = rows * lax.axis_size("batch") * lax.axis_size("mp")
    mean_loss = loss_sum / images
    grad_scale = gscale_all / images
    grad_bias = gsum_all / images
    return (mean_loss, grad_scale, grad_bias, summed[:, :embed], summed[:, embed:])


def solution(mesh):
    return jax.shard_map(
        per_device,
        mesh=mesh,
        in_specs=(
            P(("batch", "mp"), None),
            P(("batch", "mp"), None),
            P("mp", None),
            P("mp", None),
            P(),
            P(),
        ),
        out_specs=(P(), P(), P(), P("mp", None), P("mp", None)),
        check_vma=False,
    )
```

profile of v0, /device:TPU:2, one launch (start us, length us, event | category | flops | bytes accessed | tf_op | source)
XLA Modules:
  0.0 1430.0 jit_solution(16822330193604647631)
XLA Ops:
  7.2 0.0 copy-start
  7.2 0.0 all-gather.5.cloned.1.call-start
  7.2 0.7 all-gather.5.cloned.1.call-update
  7.9 0.0 all-gather.3.cloned.1.call-start
  8.0 28.2 %all-gather.5.cloned.1.call-done = bf16[768,768]{1,0:T(8,128)(2,1)} async-done(((bf16[192,768]{1,0:T(8,128)(2,1)}), bf16[768,768]{1,0:T(8,128)(2,1)}) %all-gather.5.cloned.1.call-update) | async-done | bytes 1179664 | tf_op jit(solution)/shard_map/all_gather | solution.py:47
  36.1 2.4 multiply_reduce_fusion.4
  38.5 0.2 multiply_convert_fusion.7
  38.7 2.4 collective-permute-start
  41.1 18.7 %collective-permute-done = bf16[512,768]{1,0:T(8,128)(2,1)S(1)} collective-permute-done((bf16[512,768]{1,0:T(8,128)(2,1)S(1)}, bf16[512,768]{1,0:T(8,128)(2,1)S(1)}, u32[]{:S(2)}, u32[]{:S(2)}) %collective-permute-start) | collective-permute-done | bytes 786464 | tf_op jit(solution)/shard_map/ppermute | solution.py:10
  59.9 0.0 copy-start.2
  59.9 0.1 pad_maximum_fusion.3
  60.0 1.7 collective-permute-start.1
  61.7 33.9 %collective-permute-done.1 = bf16[1024,768]{1,0:T(8,128)(2,1)S(1)} collective-permute-done((bf16[1024,768]{1,0:T(8,128)(2,1)S(1)}, bf16[1024,768]{1,0:T(8,128)(2,1)S(1)}, u32[]{:S(2)}, u32[]{:S(2)}) %collective-permute-start.1) | collective-permute-done | bytes 1572896 | tf_op jit(solution)/shard_map/ppermute | solution.py:10
  95.6 0.0 copy-done.2
  95.6 2.0 pad_maximum_fusion.2
  97.6 0.2 copy-done.4
  97.8 2.6 collective-permute-start.2
  100.4 0.0 all-gather.3.cloned.1.call-update
  100.4 0.0 reduce-scatter.4.cloned.1.call-start
  101.8 22.4 %all-gather.3.cloned.1.call-done = bf16[768,768]{1,0:T(8,128)(2,1)} async-done(((bf16[192,768]{1,0:T(8,128)(2,1)}), bf16[768,768]{1,0:T(8,128)(2,1)}) %all-gather.3.cloned.1.call-update) | async-done | bytes 1179664 | tf_op jit(solution)/shard_map/all_gather | solution.py:42
  124.2 0.0 copy-done
  124.2 2.1 multiply_reduce_fusion.5
  126.4 0.0 copy-start.5
  126.4 108.5 %collective-permute-done.2 = bf16[2048,768]{1,0:T(8,128)(2,1)} collective-permute-done((bf16[2048,768]{1,0:T(8,128)(2,1)}, bf16[2048,768]{1,0:T(8,128)(2,1)}, u32[]{:S(2)}, u32[]{:S(2)}) %collective-permute-start.2) | collective-permute-done | bytes 3145760 | tf_op jit(solution)/shard_map/ppermute | solution.py:10
  234.9 17.4 %multiply_reduce_fusion.1 = (f32[]{:T(128)}, f32[]{:T(128)}, f32[]{:T(128)}, f32[512,4096]{1,0:T(8,128)S(1)}) fusion(f32[]{:T(128)S(6)} %copy.22, f32[]{:T(128)S(6)} %exp.10, f32[]{:T(128)S(6)} %mul.102, bf16[2048,768]{1,0:T(8,128)(2,1)} %collective-permute-done.2, bf16[1024,768]{1,0:T(8,128)(2,1)} %copy-done.4, bf16[512,768]{1,0:T(8,128)(2,1)} %copy-done.2, ...), kind=kOutput, calls=%fused_computation.8 | convolution fusion | flops 3293315072 | bytes 16255000 | tf_op jit(solution)/shard_map/rd,cd->rc/dot_general | solution.py:24
  252.3 0.0 copy-start.8
  252.3 0.0 copy-done.5
  252.3 3.2 copy-done.8
  255.5 4.1 convolution_multiply_fusion
  259.6 0.0 copy-start.1
  259.6 0.4 slice.33
  260.0 4.1 copy-done.1
  264.1 0.0 collective-permute-start.3
  264.1 272.2 %collective-permute-done.3 = f32[2048,768]{1,0:T(8,128)S(1)} collective-permute-done((f32[2048,768]{1,0:T(8,128)S(1)}, f32[2048,768]{1,0:T(8,128)S(1)}, u32[]{:S(2)}, u32[]{:S(2)}) %collective-permute-start.3) | collective-permute-done | bytes 6291488 | tf_op jit(solution)/shard_map/ppermute | solution.py:10
  536.3 3.6 slice_add_fusion
  539.9 0.2 slice.35
  540.1 0.0 copy-start.3
  540.1 0.1 collective-permute-start.4
  540.2 68.2 %collective-permute-done.4 = f32[1024,768]{1,0:T(8,128)S(1)} collective-permute-done((f32[1024,768]{1,0:T(8,128)S(1)}, f32[1024,768]{1,0:T(8,128)S(1)}, u32[]{:S(2)}, u32[]{:S(2)}) %collective-permute-start.4) | collective-permute-done | bytes 3145760 | tf_op jit(solution)/shard_map/ppermute | solution.py:10
  608.4 0.4 slice_add_fusion.1
  608.8 0.1 slice.37
  608.9 0.0 copy-start.6
  608.9 2.6 collective-permute-start.5
  611.5 0.0 copy-done.3
  611.5 9.8 multiply_reduce_fusion.3
  621.3 0.0 copy-done.6
  621.3 0.0 copy-start.7
  621.3 1.1 convolution_bitcast_fusion.1
  622.4 22.0 %collective-permute-done.5 = f32[512,768]{1,0:T(8,128)S(1)} collective-permute-done((f32[512,768]{1,0:T(8,128)S(1)}, f32[512,768]{1,0:T(8,128)S(1)}, u32[]{:S(2)}, u32[]{:S(2)}) %collective-permute-start.5) | collective-permute-done | bytes 1572896 | tf_op jit(solution)/shard_map/ppermute | solution.py:10
  644.4 0.4 multiply_reduce_fusion.2
  644.9 0.0 copy-done.7
  644.9 1.1 convolution_bitcast_fusion
  646.0 2.5 pad_maximum_fusion.1
  648.5 6.1 copy.18
  654.5 0.0 reduce-scatter.4.cloned.1.call-update
  654.5 0.0 all-reduce.3.cloned.1.call-start
  654.6 55.0 %reduce-scatter.4.cloned.1.call-done = f32[192,1536]{1,0:T(8,128)} async-done(((f32[768,1536]{1,0:T(8,128)}), f32[192,1536]{1,0:T(8,128)}) %reduce-scatter.4.cloned.1.call-update) | async-done | bytes 1179664
  709.6 2.9 copy.19
  712.5 0.0 all-reduce.3.cloned.1.call-update
  713.1 78.3 %all-reduce = (f32[]{:T(128)}, f32[]{:T(128)}, f32[]{:T(128)}) all-reduce(f32[]{:T(128)S(6)} %div.21, f32[]{:T(128)} %get-tuple-element.17, f32[]{:T(128)} %get-tuple-element.15), channel_id=1, replica_groups=mesh['batch'=64,'mp'=4] {'batch','mp'}, use_global_device_ids=true, to_apply=%region_3.4 | all-reduce | flops 3 | bytes 24 | tf_op jit(solution)/shard_map/psum | solution.py:82
  793.4 623.1 %all-reduce.3.cloned.1.call-done = f32[192,1536]{0,1:T(8,128)} async-done(((f32[192,1536]{0,1:T(8,128)}), f32[192,1536]{0,1:T(8,128)}) %all-reduce.3.cloned.1.call-update) | async-done | bytes 1179664 | tf_op jit(solution)/shard_map/psum | solution.py:81
  1416.5 1.5 fusion.12
  1418.0 1.1 copy.16
  1419.1 1.1 copy.15
  (3 shorter events, 0.0 us)
Async XLA Ops:
  7.2 117.1 %copy-start = (bf16[512,768]{1,0:T(8,128)(2,1)S(1)}, bf16[512,768]{1,0:T(8,128)(2,1)}, u32[]{:S(2)}) copy-start(bf16[512,768]{1,0:T(8,128)(2,1)} %param.6) | copy-start | bytes 2359300
  7.2 29.0 %all-gather.5.cloned.1.call-start = ((), (), s32[]{:S(2)}) async-start(), calls=%async_computation.2 | async-start | bytes 1474560 | tf_op jit(solution)/shard_map/all_gather | solution.py:47
  7.9 116.3 %all-gather.3.cloned.1.call-start = ((), (), s32[]{:S(2)}) async-start(), calls=%async_computation.1 | async-start | bytes 1474560 | tf_op jit(solution)/shard_map/all_gather | solution.py:42
  38.7 21.2 %collective-permute-start = (bf16[512,768]{1,0:T(8,128)(2,1)S(1)}, bf16[512,768]{1,0:T(8,128)(2,1)S(1)}, u32[]{:S(2)}, u32[]{:S(2)}) collective-permute-start(bf16[512,768]{1,0:T(8,128)(2,1)S(1)} %multiply_convert_fusion.7), channel_id=1, source_target_pairs={{0,4},{4,0},{8,12},{12,8},{16,20},{20,16},{24,28},{28,24},{32,36},... | collective-permute-start | bytes 2359304 | tf_op jit(solution)/shard_map/ppermute | solution.py:10
  59.9 35.8 %copy-start.2 = (bf16[512,768]{1,0:T(8,128)(2,1)}, bf16[512,768]{1,0:T(8,128)(2,1)S(1)}, u32[]{:S(2)}) copy-start(bf16[512,768]{1,0:T(8,128)(2,1)S(1)} %collective-permute-done) | copy-start | bytes 2359300
  60.0 35.7 %collective-permute-start.1 = (bf16[1024,768]{1,0:T(8,128)(2,1)S(1)}, bf16[1024,768]{1,0:T(8,128)(2,1)S(1)}, u32[]{:S(2)}, u32[]{:S(2)}) collective-permute-start(bf16[1024,768]{1,0:T(8,128)(2,1)S(1)} %pad_maximum_fusion.3), channel_id=1, source_target_pairs={{0,8},{4,12},{8,0},{12,4},{16,24},{20,28},{24,16},{28,20},{32,40},... | collective-permute-start | bytes 4718600 | tf_op jit(solution)/shard_map/ppermute | solution.py:10
  95.6 2.2 copy-start.4
  97.8 137.0 %collective-permute-start.2 = (bf16[2048,768]{1,0:T(8,128)(2,1)}, bf16[2048,768]{1,0:T(8,128)(2,1)}, u32[]{:S(2)}, u32[]{:S(2)}) collective-permute-start(bf16[2048,768]{1,0:T(8,128)(2,1)} %pad_maximum_fusion.2), channel_id=1, source_target_pairs={{0,16},{4,20},{8,24},{12,28},{16,0},{20,4},{24,8},{28,12},{32,48},... | collective-permute-start | bytes 9437192 | tf_op jit(solution)/shard_map/ppermute | solution.py:10
  100.4 609.1 %reduce-scatter.4.cloned.1.call-start = ((), (), s32[]{:S(2)}) async-start(), calls=%async_computation.4 | async-start | bytes 5898240
  126.4 125.9 %copy-start.5 = (f32[512,768]{1,0:T(8,128)}, f32[512,768]{1,0:T(8,128)S(1)}, u32[]{:S(2)}) copy-start(f32[512,768]{1,0:T(8,128)S(1)} %get-tuple-element.26) | copy-start | bytes 4718596
  252.3 3.2 copy-start.8
  259.6 4.6 copy-start.1
  264.1 272.2 %collective-permute-start.3 = (f32[2048,768]{1,0:T(8,128)S(1)}, f32[2048,768]{1,0:T(8,128)S(1)}, u32[]{:S(2)}, u32[]{:S(2)}) collective-permute-start(f32[2048,768]{1,0:T(8,128)S(1)} %slice.33), channel_id=1, source_target_pairs={{0,16},{4,20},{8,24},{12,28},{16,0},{20,4},{24,8},{28,12},{32,48},... | collective-permute-start | bytes 18874376 | tf_op jit(solution)/shard_map/ppermute | solution.py:10
  540.1 71.4 %copy-start.3 = (bf16[512,768]{1,0:T(8,128)(2,1)S(1)}, bf16[512,768]{1,0:T(8,128)(2,1)}, u32[]{:S(2)}) copy-start(bf16[512,768]{1,0:T(8,128)(2,1)} %copy-done.2) | copy-start | bytes 2359300
  540.1 68.3 %collective-permute-start.4 = (f32[1024,768]{1,0:T(8,128)S(1)}, f32[1024,768]{1,0:T(8,128)S(1)}, u32[]{:S(2)}, u32[]{:S(2)}) collective-permute-start(f32[1024,768]{1,0:T(8,128)S(1)} %slice.35), channel_id=1, source_target_pairs={{0,8},{4,12},{8,0},{12,4},{16,24},{20,28},{24,16},{28,20},{32,40},... | collective-permute-start | bytes 9437192 | tf_op jit(solution)/shard_map/ppermute | solution.py:10
  608.9 12.4 copy-start.6
  608.9 35.5 %collective-permute-start.5 = (f32[512,768]{1,0:T(8,128)S(1)}, f32[512,768]{1,0:T(8,128)S(1)}, u32[]{:S(2)}, u32[]{:S(2)}) collective-permute-start(f32[512,768]{1,0:T(8,128)S(1)} %slice.37), channel_id=1, source_target_pairs={{0,4},{4,0},{8,12},{12,8},{16,20},{20,16},{24,28},{28,24},{32,36},... | collective-permute-start | bytes 4718600 | tf_op jit(solution)/shard_map/ppermute | solution.py:10
  621.3 23.5 %copy-start.7 = (bf16[512,768]{1,0:T(8,128)(2,1)S(1)}, bf16[512,768]{1,0:T(8,128)(2,1)}, u32[]{:S(2)}) copy-start(bf16[512,768]{1,0:T(8,128)(2,1)} %param.7) | copy-start | bytes 2359300
  654.5 762.0 %all-reduce.3.cloned.1.call-start = ((), (), s32[]{:S(2)}) async-start(), calls=%async_computation.3 | async-start | bytes 3145728 | tf_op jit(solution)/shard_map/psum | solution.py:81
Sparse Core Ops, SparseCore 0:
  9.8 26.3 all-gather.4
  100.5 23.6 all-gather.2
  654.7 54.8 reduce-scatter.3
  712.6 703.8 all-reduce.2
where the time goes:
time: 1430 us
  waiting for transfers between devices  1250 us (87%)
  blocking collectives  78.3 us (5%)
  matrix products  38 us (3%)
  between operations  21.2 us (1%)
  local copies, waits for them, and re-layouts  20.8 us (1%)
    psum x1, waiting for transfers between devices, per_device(): summed = lax.psum(local_rows, 'batch')  623 us
    ppermute x6, waiting for transfers between devices, from_partner(): lax.ppermute(value, axis, [(i, i ^ 1 << bit) for i in range(lax.axis_size...  524 us
    psum x1, blocking collectives, per_device(): lax.psum((loss, gsum, gscale), ('batch', 'mp'))  78.3 us
    unnamed x5, waiting for transfers between devices  55.7 us
  transfers between devices with their start and end apart: 10, of which 10 were waited for; matrix products, arithmetic and copies ran while one was open for 1% of the time, Pallas kernels for 0%

commit v1 on v0

v1 whole, which is shorter than its diff:
```python
import functools

import jax
import jax.numpy as jnp
from jax import lax
from jax.experimental import pallas as pl
from jax.experimental.pallas import tpu as pltpu
from jax.sharding import PartitionSpec as P

MESH = pl.DeviceIdType.MESH
BF, F32 = jnp.bfloat16, jnp.float32
TXT, IMG = 0, 1
NC = 2
TR = 256


def kernel(dims, ls_ref, bias_ref, imgf, txtf, wi, wt, out_txt, out_img, out_s,
           w, zt, zi, zf, rr, d_t, d_i, st, rt, si, ri, sz, rz,
           p, r0, sx, rx, bb, cz, cy, oo, acc, s0, s1, s2, s3, send, recv):
    rows, embed, shard, width, images = dims
    feats = (txtf, imgf)
    b, m = lax.axis_index("batch"), lax.axis_index("mp")
    xh, z, y = b % 2, (b // 2) % 8, b // 16
    xl, c = m // 2, m % 2
    x = xh * 2 + xl

    def at(xx, yy, zz, cc):
        return ((yy * 8 + zz) * 2 + xx // 2, (xx % 2) * 2 + cc)

    partner = at(x, y, z, 1 - c)
    xs = [at((x + k) % 4, y, z, c) for k in (1, 2, 3)]
    zs = [at(x, y, (z + k) % 8, c) for k in range(1, 8)]
    ys = [at(x, (y + k) % 4, z, c) for k in (1, 2, 3)]
    x2 = xs[1]
    z1 = at(x, y, z + 1 - 2 * (z % 2), c)
    z2 = at(x, y, z + 2 - 4 * ((z // 2) % 2), c)

    barrier = pltpu.get_barrier_semaphore()
    peers = [partner] + xs + zs + ys
    for peer in peers:
        pl.semaphore_signal(barrier, inc=1, device_id=peer, device_id_type=MESH)
    pl.semaphore_wait(barrier, len(peers))

    started = []

    def post(src, dst, peer):
        n = len(started)
        copy = pltpu.make_async_remote_copy(
            src_ref=src, dst_ref=dst, send_sem=send.at[n], recv_sem=recv.at[n],
            device_id=peer, device_id_type=MESH)
        started.append(copy)
        copy.start()
        return copy

    def part(start, size, multiple):
        return pl.ds(pl.multiple_of(start, multiple), size)

    half = shard // 2
    ws = (wt, wi)
    own = [None, None]
    for k in (TXT, IMG):
        mine = m * shard
        own[k] = (
            post(ws[k].at[pl.ds(0, half)], w.at[k, part(mine, half, 16)], xs[0]),
            post(ws[k].at[pl.ds(half, half)], w.at[k, part(mine + half, half, 16)], xs[2]),
            post(ws[k], w.at[k, part(mine, shard, 16)], partner),
        )
    for k in (TXT, IMG):
        w[k, part(m * shard, shard, 16), :] = ws[k][...]
    across = ((1 - xl) * 2 + c) * shard
    passed = [None, None]
    for k in (TXT, IMG):
        own[k][0].wait_recv()
        own[k][1].wait_recv()
        there = w.at[k, part(across, shard, 16)]
        passed[k] = post(there, there, partner)

    acc[...] = jnp.zeros_like(acc)
    scale = jnp.exp(jnp.full((1, embed), ls_ref[0], F32))
    bias = bias_ref[0]
    cr = rows // NC

    def project(k, zall, sends):
        own[k][2].wait_recv()
        passed[k].wait_recv()
        for q in range(NC):
            here = pl.ds(q * cr, cr)
            u = jnp.dot(feats[k][here, :], w[k], preferred_element_type=F32)
            r = lax.rsqrt(jnp.sum(u * u, axis=1, keepdims=True) + 1e-06)
            v = u * r
            zf[k, here, :] = v
            rr[k, here, :] = jnp.broadcast_to(r, (cr, 128))
            zall[0, here, :] = v.astype(BF)
            sends(q, here)

    t_z, t_x, i_z, t_d = [], [], [], []

    def send_txt(q, here):
        t_z.append(post(zt.at[0, here], zt.at[1, here], z1))
        t_x.append(post(zt.at[0, here], zt.at[2, here], x2))

    def send_img(q, here):
        i_z.append(post(zi.at[0, here], zi.at[1, here], z2))

    project(TXT, zt, send_txt)
    project(IMG, zi, send_img)

    def pairs(i, t):
        first_i, first_t = t == 0, i == 0

        def tile(n, carry):
            here = part(n * TR, TR, TR)
            left = zi[i, here, :]
            s = lax.dot_general(left, zt[t], (((1,), (1,)), ((), ())), preferred_element_type=F32)
            logit = scale[:, :rows] * s + bias
            if i == 0 and t == 0:
                row_ids = lax.broadcasted_iota(jnp.int32, s.shape, 0) + n * TR
                col_ids = lax.broadcasted_iota(jnp.int32, s.shape, 1)
                pair = row_ids == col_ids
                logit = jnp.where(pair, -logit, logit)
            e = jnp.exp(-jnp.abs(logit))
            inv = 1.0 / (1.0 + e)
            term = jnp.maximum(logit, 0.0) + jnp.log1p(e)
            g = jnp.where(logit >= 0.0, inv, e * inv)
            if i == 0 and t == 0:
                g = jnp.where(pair, -g, g)
            g = g * (1.0 / width)
            acc[0:1, :] += jnp.sum(term, axis=0, keepdims=True)
            acc[1:2, :] += jnp.sum(g, axis=0, keepdims=True)
            acc[2:3, :] += jnp.sum(g * s, axis=0, keepdims=True)
            gb = g.astype(BF)
            to_i = jnp.dot(gb, zt[t], preferred_element_type=F32)
            to_t = lax.dot_general(gb, left, (((0,), (0,)), ((), ())), preferred_element_type=F32)
            if first_i:
                d_i[i, here, :] = to_i
            else:
                d_i[i, here, :] += to_i
            if first_t:
                @pl.when(n == 0)
                def _():
                    d_t[t] = to_t

                @pl.when(n > 0)
                def _():
                    d_t[t] += to_t
            else:
                d_t[t] += to_t
            return carry

        lax.fori_loop(0, rows // TR, tile, 0)

    pairs(0, 0)
    for q in range(NC):
        here = pl.ds(q * cr, cr)
        t_z[q].wait_recv()
        t_d.append(post(zt.at[1, here], zt.at[3, here], x2))
    pairs(0, 1)
    for q in range(NC):
        t_x[q].wait_recv()
    pairs(0, 2)
    for q in range(NC):
        i_z[q].wait_recv()
    pairs(1, 0)
    pairs(1, 2)
    b_x = [[], []]
    for q in range(NC):
        here = pl.ds(q * cr, cr)
        st[0, here, :] = d_t[2, here, :].astype(BF)
        b_x[0].append(post(st.at[0, here], rt.at[0, here], x2))
    pairs(1, 1)
    for q in range(NC):
        t_d[q].wait_recv()
    pairs(0, 3)
    pairs(1, 3)
    b_i, b_z = [], []
    for q in range(NC):
        here = pl.ds(q * cr, cr)
        st[1, here, :] = d_t[3, here, :].astype(BF)
        b_x[1].append(post(st.at[1, here], rt.at[1, here], x2))
        si[here, :] = d_i[1, here, :].astype(BF)
        b_i.append(post(si.at[here], ri.at[here], z2))
    row = acc[...]
    s0[0] = row[:, 0:128] + row[:, 128:256] + row[:, 256:384] + row[:, 384:512]

    def back(k, dz):
        v, r = zf[k], rr[k][:, 0:1]
        dz = scale * dz
        du = (r * (dz - v * jnp.sum(v * dz, axis=1, keepdims=True))).astype(BF)
        p[k] = lax.dot_general(feats[k][...], du, (((0,), (0,)), ((), ())), preferred_element_type=F32)

    def core_send(k):
        return [post(p.at[k, part((2 * h + 1 - c) * shard, shard, 8)], r0.at[k, h], partner) for h in (0, 1)]

    def x_send(k, arrived):
        for a in arrived:
            a.wait_recv()
        copies = []
        for n in range(3):
            xx = (x + n + 1) % 4
            lo, hi = xx % 2, xx // 2
            sx[k, n] = (p[k, part((2 * lo + c) * shard + hi * half, half, 8), :]
                        + r0[k, lo, part(hi * half, half, 8), :]).astype(sx.dtype)
            copies.append(post(sx.at[k, n], rx.at[k, n], xs[n]))
        bb[k] = p[k, part(m * shard + xh * half, half, 8), :] + r0[k, xl, part(xh * half, half, 8), :]
        return copies

    zr, zc = half // 4, embed // 2

    def corner(zz):
        return part((zz // 2) * zr, zr, 8), part((zz % 2) * zc, zc, 128)

    def z_send(k, arrived):
        for a in arrived:
            a.wait_recv()
        bb[k] = bb[k] + (rx[k, 0].astype(F32) + rx[k, 1].astype(F32) + rx[k, 2].astype(F32))
        copies = []
        for n in range(7):
            i, j = corner((z + n + 1) % 8)
            copies.append(post(bb.at[k, i, j], cz.at[k, n], zs[n]))
        return copies

    def y_send(k, arrived):
        for a in arrived:
            a.wait_recv()
        i, j = corner(z)
        total = bb[k, i, j]
        for n in range(7):
            total = total + cz[k, n]
        cy[k, y] = total
        return [post(cy.at[k, y], cy.at[k, y], ys[n]) for n in range(3)]

    def z_gather(k, arrived):
        for a in arrived:
            a.wait_recv()
        i, j = corner(z)
        i = part(xh * half + (z // 2) * zr, zr, 8)
        oo[k, i, j] = (cy[k, 0] + cy[k, 1]) + (cy[k, 2] + cy[k, 3])
        here = oo.at[k, i, j]
        return [post(here, here, zs[n]) for n in range(7)]

    def x_gather(k, arrived):
        for a in arrived:
            a.wait_recv()
        here = oo.at[k, part(xh * half, half, 8)]
        return [post(here, here, x2)]

    a_s = [post(s0.at[0], s0.at[1], partner)]

    for q in range(NC):
        here = pl.ds(q * cr, cr)
        b_x[1][q].wait_recv()
        sz[here, :] = (d_t[1, here, :] + rt[1, here, :].astype(F32)).astype(BF)
        b_z.append(post(sz.at[here], rz.at[here], z1))
    for q in range(NC):
        b_i[q].wait_recv()
    back(IMG, d_i[0] + ri[...].astype(F32))
    a_i = core_send(IMG)
    a_s[0].wait_recv()
    s1[x] = s0[0] + s0[1]
    a_s = [post(s1.at[x], s1.at[x], peer) for peer in xs]
    a_i = x_send(IMG, a_i)
    for q in range(NC):
        b_x[0][q].wait_recv()
        b_z[q].wait_recv()
    back(TXT, d_t[0] + rt[0].astype(F32) + rz[...].astype(F32))
    a_t = core_send(TXT)
    a_t = x_send(TXT, a_t)
    a_i = z_send(IMG, a_i)
    for a in a_s:
        a.wait_recv()
    s2[z] = (s1[0] + s1[1]) + (s1[2] + s1[3])
    a_s = [post(s2.at[z], s2.at[z], peer) for peer in zs]
    a_t = z_send(TXT, a_t)
    a_i = y_send(IMG, a_i)
    for a in a_s:
        a.wait_recv()
    total = s2[0]
    for n in range(1, 8):
        total = total + s2[n]
    s3[y] = total
    a_s = [post(s3.at[y], s3.at[y], peer) for peer in ys]
    a_t = y_send(TXT, a_t)
    a_i = z_gather(IMG, a_i)
    a_t = z_gather(TXT, a_t)
    a_i = x_gather(IMG, a_i)
    a_t = x_gather(TXT, a_t)
    for a in a_s:
        a.wait_recv()
    total = jnp.sum((s3[0] + s3[1]) + (s3[2] + s3[3]), axis=1, keepdims=True) * (1.0 / images)
    kind = lax.broadcasted_iota(jnp.int32, (8, 128), 0)
    total = jnp.broadcast_to(total, (8, 128))
    total = jnp.where(kind == 0, total * (1.0 / width), total)
    out_s[...] = jnp.where(kind == 2, total * scale[:, 0:128], total)
    a_i[0].wait_recv()
    out_img[...] = oo[IMG]
    a_t[0].wait_recv()
    out_txt[...] = oo[TXT]
    for copy in started:
        copy.wait_send()


def per_device(img_feat, txt_feat, img_proj, txt_proj, logit_scale, bias):
    rows, embed = img_feat.shape
    shard = img_proj.shape[0]
    width = rows * 8
    images = rows * lax.axis_size("batch") * lax.axis_size("mp")
    half = shard // 2
    ar = F32
    v = pltpu.VMEM
    scratch = [
        v((2, embed, embed), BF),
        v((4, rows, embed), BF), v((2, rows, embed), BF),
        v((2, rows, embed), F32), v((2, rows, 128), F32),
        v((4, rows, embed), F32), v((2, rows, embed), F32),
        v((2, rows, embed), BF), v((2, rows, embed), BF),
        v((rows, embed), BF), v((rows, embed), BF),
        v((rows, embed), BF), v((rows, embed), BF),
        v((2, embed, embed), F32), v((2, 2, shard, embed), F32),
        v((2, 3, half, embed), ar), v((2, 3, half, embed), ar),
        v((2, half, embed), F32), v((2, 7, half // 4, embed // 2), F32),
        v((2, 4, half // 4, embed // 2), F32), v((2, shard, embed), F32),
        v((8, rows), F32),
        v((2, 8, 128), F32), v((4, 8, 128), F32), v((8, 8, 128), F32), v((4, 8, 128), F32),
        pltpu.SemaphoreType.DMA((96,)), pltpu.SemaphoreType.DMA((96,)),
    ]
    vm = pl.BlockSpec(memory_space=pltpu.VMEM)
    sm = pl.BlockSpec(memory_space=pltpu.SMEM)
    g_txt, g_img, s = pl.pallas_call(
        functools.partial(kernel, (rows, embed, shard, width, images)),
        out_shape=(
            jax.ShapeDtypeStruct((shard, embed), F32),
            jax.ShapeDtypeStruct((shard, embed), F32),
            jax.ShapeDtypeStruct((8, 128), F32),
        ),
        in_specs=[sm, sm, vm, vm, vm, vm],
        out_specs=(vm, vm, vm),
        scratch_shapes=scratch,
        compiler_params=pltpu.CompilerParams(
            collective_id=0, has_side_effects=True, vmem_limit_bytes=64 * 1024 * 1024 - 65536),
    )(logit_scale.reshape(1), bias.reshape(1), img_feat, txt_feat, img_proj, txt_proj)
    return s[0, 0], s[2, 0], s[1, 0], g_img, g_txt


def solution(mesh):
    return jax.shard_map(
        per_device,
        mesh=mesh,
        in_specs=(
            P(("batch", "mp"), None),
            P(("batch", "mp"), None),
            P("mp", None),
            P("mp", None),
            P(),
            P(),
        ),
        out_specs=(P(), P(), P(), P("mp", None), P("mp", None)),
        check_vma=False,
    )
```

time: 1430 us -> 178 us (0.12)
  waiting for transfers between devices: 1250 us -> 0 us
  Pallas kernels: 0 us -> 170 us
  blocking collectives: 78.3 us -> 0 us
  matrix products: 38 us -> 0 us
  between operations: 21.2 us -> 1.94 us
  local copies, waits for them, and re-layouts: 20.8 us -> 4.11 us
    psum x1 -> x0, waiting for transfers between devices: 623 us -> none  [per_device(): summed = lax.psum(local_rows, 'batch')]
    ppermute x6 -> x0, waiting for transfers between devices: 524 us -> none  [from_partner(): lax.ppermute(value, axis, [(i, i ^ 1 << bit) for i in range(lax.axis_size...]
    pallas_call x0 -> x1, Pallas kernels: none -> 170 us  [per_device(): pl.pallas_call(functools.partial(kernel, (rows, embed, shard, width, imag...]
    psum x1 -> x0, blocking collectives: 78.3 us -> none  [per_device(): lax.psum((loss, gsum, gscale), ('batch', 'mp'))]
    unnamed x5 -> x0, waiting for transfers between devices: 55.7 us -> none
    all_gather x2 -> x0, waiting for transfers between devices: 50.6 us -> none  [the longest x1 28.2 us: per_device(): lax.all_gather(txt_proj, 'mp', axis=0, tiled=True)]
    dot_general x7 -> x0, matrix products: 38 us -> none  [the longest x1 17.4 us: pair_terms(): jnp.einsum('rd,cd->rc', left, right, preferred_element_type=jnp.float32)]
    unnamed x22 -> x4, local copies, waits for them, and re-layouts: 18.7 us -> 2.8 us
  transfers between devices with their start and end apart: 10 -> 0, of which waited for: 10 -> 0; matrix products, arithmetic and copies ran while one was open for 1% -> 0% of each run, Pallas kernels for 0% -> 0%
where the time goes in v1:
time: 178 us; the launch traced here: 176 us
  Pallas kernels  170 us (96%)
  local copies, waits for them, and re-layouts  4.11 us (2%)
  between operations  1.94 us (1%)
    pallas_call x1, Pallas kernels, per_device(): pl.pallas_call(functools.partial(kernel, (rows, embed, shard, width, imag...  170 us

profile of v1, /device:TPU:2, one launch (start us, length us, event | category | flops | bytes accessed | tf_op | source)
XLA Modules:
  0.0 176.3 jit_solution(4772722441971600466)
XLA Ops:
  1.9 170.3 %shard_map.101 = (f32[192,768]{1,0:T(8,128)}, f32[192,768]{1,0:T(8,128)}, f32[8,128]{1,0:T(8,128)}) custom-call(f32[1]{0:T(128)} %bitcast.5.ls_ref, f32[1]{0:T(128)} %bitcast.6.bias_ref, bf16[512,768]{1,0:T(8,128)(2,1)} %imgf.1, bf16[512,768]{1,0:T(8,128)(2,1)} %txtf.1, bf16[192,768]{1,0:T(8,128)(2,1)} %wi.1, bf16[192,768]{1,0:T(8,128)(2,1)} %wt.1), custom_call_target="tpu_custom_call" | custom-call | tf_op jit(solution)/shard_map/pallas_call | solution.py:328
  172.2 1.3 fusion
  173.5 0.0 copy-start
  173.6 2.0 %copy.15 = f32[192,768]{1,0:T(8,128)} copy(f32[192,768]{1,0:T(8,128)} %get-tuple-element.22) | data formatting | bytes 1179648
  175.5 0.0 copy-done
  175.5 0.8 copy.16
Async XLA Ops:
  173.5 2.0 %copy-start = (f32[192,768]{1,0:T(8,128)S(1)}, f32[192,768]{1,0:T(8,128)}, u32[]{:S(2)}) copy-start(f32[192,768]{1,0:T(8,128)} %get-tuple-element.23) | copy-start | bytes 1769476

commit v2 on v0

v2 whole, which is shorter than its diff:
```python
import functools

import jax
import jax.numpy as jnp
from jax import lax
from jax.experimental import pallas as pl
from jax.experimental.pallas import tpu as pltpu
from jax.sharding import PartitionSpec as P

MESH = pl.DeviceIdType.MESH
BF, F32 = jnp.bfloat16, jnp.float32
TXT, IMG = 0, 1


def kernel(dims, ls_ref, bias_ref, imgf, txtf, wi, wt, out_txt, out_img, out_s,
           w, ft, zt, zi, zf, rr, d_t, d_i, st, rt, si, ri, sz, rz,
           p, r0, sx, rx, bb, r2, zb, cz, acc, s0, s1, s2, s3, send, recv):
    rows, embed, shard, width, images = dims
    feats = (txtf, imgf)
    outs = (out_txt, out_img)
    b, m = lax.axis_index("batch"), lax.axis_index("mp")
    xh, z, y = b % 2, (b // 2) % 8, b // 16
    xl, c = m // 2, m % 2
    x = xh * 2 + xl

    def at(xx, yy, zz, cc):
        return ((yy * 8 + zz) * 2 + xx // 2, (xx % 2) * 2 + cc)

    partner = at(x, y, z, 1 - c)
    xs = [at((x + k) % 4, y, z, c) for k in (1, 2, 3)]
    zs = [at(x, y, (z + k) % 8, c) for k in range(1, 8)]
    ys = [at(x, (y + k) % 4, z, c) for k in (1, 2, 3)]
    x2 = xs[1]
    z1 = at(x, y, z + 1 - 2 * (z % 2), c)
    z2 = at(x, y, z + 2 - 4 * ((z // 2) % 2), c)

    barrier = pltpu.get_barrier_semaphore()
    peers = [partner] + xs + zs + ys
    for peer in peers:
        pl.semaphore_signal(barrier, inc=1, device_id=peer, device_id_type=MESH)
    for k in (TXT, IMG):
        ft[k] = feats[k][...].T
    acc[...] = jnp.zeros_like(acc)
    d_i[...] = jnp.zeros_like(d_i)
    d_t[...] = jnp.zeros_like(d_t)
    pl.semaphore_wait(barrier, len(peers))

    started = []

    def post(src, dst, peer):
        n = len(started)
        copy = pltpu.make_async_remote_copy(
            src_ref=src, dst_ref=dst, send_sem=send.at[n], recv_sem=recv.at[n],
            device_id=peer, device_id_type=MESH)
        started.append(copy)
        copy.start()
        return copy

    def part(start, size, multiple):
        return pl.ds(pl.multiple_of(start, multiple), size)

    def wait(copies):
        for copy in copies:
            copy.wait_recv()

    half = shard // 2
    ws = (wt, wi)
    own = [None, None]
    mine = m * shard
    for k in (TXT, IMG):
        own[k] = (
            post(ws[k].at[pl.ds(0, half)], w.at[k, part(mine, half, 16)], xs[0]),
            post(ws[k].at[pl.ds(half, half)], w.at[k, part(mine + half, half, 16)], xs[2]),
            post(ws[k], w.at[k, part(mine, shard, 16)], partner),
        )
    for k in (TXT, IMG):
        w[k, part(mine, shard, 16), :] = ws[k][...]
    scale = jnp.exp(jnp.full((1, embed), ls_ref[0], F32))
    bias = bias_ref[0]
    across = ((1 - xl) * 2 + c) * shard
    CR = rows // 2

    def fetch(k):
        wait(own[k][:2])
        there = w.at[k, part(across, shard, 16)]
        return post(there, there, partner)

    def project(k, passed, zall, sends):
        wait([own[k][2], passed])
        for q in range(2):
            here = pl.ds(q * CR, CR)
            u = jnp.dot(feats[k][here, :], w[k], preferred_element_type=F32)
            r = lax.rsqrt(jnp.sum(u * u, axis=1, keepdims=True) + 1e-06)
            v = u * r
            zf[k, here, :] = v
            rr[k, here, :] = jnp.broadcast_to(r, (CR, 128))
            zall[here, :] = v.astype(BF)
            sends(here)

    def unit(n, q=0):
        return pl.ds(n * rows + q * CR, CR)

    t_z, t_x, i_z, t_d = [], [], [], []
    fine = CR // 2

    def small(n, q):
        return pl.ds(n * rows + q * fine, fine)

    def next_txt():
        q = len(t_z)
        t_z.append(post(zt.at[small(0, q)], zt.at[small(1, q)], z2))

    def next_img():
        q = len(i_z)
        i_z.append(post(zi.at[small(0, q)], zi.at[small(1, q)], z1))

    def send_txt(here):
        q = len(t_x)
        if q == 0:
            next_txt()
            next_txt()
        t_x.append(post(zt.at[here], zt.at[unit(2, q)], x2))

    passed_t = fetch(TXT)
    project(TXT, passed_t, zt, send_txt)
    passed_i = fetch(IMG)
    project(IMG, passed_i, zi, lambda here: None)
    next_img()
    next_txt()
    next_img()
    next_txt()
    next_img()
    next_img()

    def fold(a):
        return jnp.sum(a.reshape(a.shape[0] // 8, 8, a.shape[1]), axis=0)

    def tile(i0, ni, t0, nt, own_pairs=False):
        hi, ht = part(i0, ni, CR), part(t0, nt, CR)
        left, right = zi[hi, :], zt[ht, :]
        s = lax.dot_general(left, right, (((1,), (1,)), ((), ())), preferred_element_type=F32)
        logit = scale[:, :nt] * s + bias
        if own_pairs:
            row_ids = lax.broadcasted_iota(jnp.int32, s.shape, 0) + i0
            col_ids = lax.broadcasted_iota(jnp.int32, s.shape, 1) + t0
            pair = row_ids == col_ids
            logit = jnp.where(pair, -logit, logit)
        e = jnp.exp(logit)
        more = 1.0 + e
        g = e / (more * width)
        if own_pairs:
            g = jnp.where(pair, -g, g)
        term = fold(jnp.log(more[: ni // 2] * more[ni // 2:]))
        gsum, gs = fold(g), fold(g * s)
        for n in range(nt // CR):
            cols = slice(n * CR, n * CR + CR)
            acc[0] += term[:, cols]
            acc[1] += gsum[:, cols]
            acc[2] += gs[:, cols]
        gb = g.astype(BF)
        d_i[hi, :] += jnp.dot(gb, right, preferred_element_type=F32)
        d_t[ht, :] += lax.dot_general(gb, left, (((0,), (0,)), ((), ())), preferred_element_type=F32)

    def loop(count, body):
        def step(n, carry):
            body(n)
            return carry

        lax.fori_loop(0, count, step, 0)

    def relay(q):
        wait(t_z[2 * q:2 * q + 2])
        t_d.append(post(zt.at[unit(1, q)], zt.at[unit(3, q)], x2))

    loop(2, lambda n: tile(n * CR, CR, 0, rows, True))
    relay(0)
    wait(t_x)
    loop(2, lambda n: tile(n * CR, CR, 2 * rows, rows))
    relay(1)
    loop(2, lambda n: tile(n * CR, CR, rows, rows))
    wait(i_z[:2])
    loop(3, lambda n: tile(rows, CR, n * rows, rows))
    wait([t_d[0]])
    loop(3, lambda n: tile(n * CR, CR, 3 * rows, CR))
    wait(i_z[2:])
    tile(rows + CR, CR, 2 * rows, rows)
    b_2, b_3, b_i, b_z = [], [], [], []

    def send_2(q):
        here = pl.ds(q * CR, CR)
        st[here, :] = d_t[unit(2, q), :].astype(BF)
        b_2.append(post(st.at[here], rt.at[here], x2))

    def send_3(q):
        for n in (2 * q, 2 * q + 1):
            here = pl.ds(rows + n * fine, fine)
            st[here, :] = d_t[small(3, n), :].astype(BF)
            b_3.append(post(st.at[here], rt.at[here], x2))

    def send_i(q):
        here = pl.ds(q * fine, fine)
        si[here, :] = d_i[small(1, q), :].astype(BF)
        b_i.append(post(si.at[here], ri.at[here], z1))

    send_2(0)
    tile(rows + CR, CR, 3 * rows, CR)
    send_3(0)
    loop(2, lambda n: tile(rows + CR, CR, n * rows, rows))
    wait([t_d[1]])
    loop(4, lambda n: tile(n * CR, CR, 3 * rows + CR, CR))
    send_3(1)
    send_2(1)
    for q in range(4):
        send_i(q)
    s0[0] = acc[:, :, 0:128] + acc[:, :, 128:256]
    a_s = [post(s0.at[0], s0.at[1], partner)]

    hc = embed // 2
    zr = half // 4

    def back(k, dz):
        v, r = zf[k], rr[k][:, 0:1]
        dz = scale * dz
        du = (r * (dz - v * jnp.sum(v * dz, axis=1, keepdims=True))).astype(BF)
        copies = []
        for j in (0, 1):
            cols = pl.ds(j * hc, hc)
            p[k, :, cols] = lax.dot_general(
                ft[k], du[:, j * hc:(j + 1) * hc], (((1,), (0,)), ((), ())), preferred_element_type=F32)
            copies.append([
                post(p.at[k, part((2 * h + 1 - c) * shard, shard, 8), cols], r0.at[k, h, :, cols], partner)
                for h in (0, 1)])
        return copies

    def block(k, j, yy, xx):
        cols = pl.ds(j * hc, hc)
        if j == 0:
            q = shard // 4
            return jnp.concatenate([
                p[k, part((2 * h + c) * shard + yy * q, q, 8), cols] + r0[k, h, part(yy * q, q, 8), cols]
                for h in (0, 1)], axis=0)
        lo, hi = xx % 2, xx // 2
        return (p[k, part((2 * lo + c) * shard + hi * half, half, 8), cols]
                + r0[k, lo, part(hi * half, half, 8), cols])

    def first(k, j, arrived):
        wait(arrived)
        copies = []
        for n in range(3):
            sx[k, j, n] = block(k, j, (y + n + 1) % 4, (x + n + 1) % 4)
            copies.append(post(sx.at[k, j, n], rx.at[k, j, n], (ys, xs)[j][n]))
        bb[k, j] = block(k, j, y, x)
        return copies

    def second(k, j, arrived):
        wait(arrived)
        bb[k, j] = bb[k, j] + (rx[k, j, 0] + rx[k, j, 1] + rx[k, j, 2])
        copies = []
        for n in range(3):
            xx, yy = (x + n + 1) % 4, (y + n + 1) % 4
            at_row = (xx % 2) * (2 * zr) + (xx // 2) * zr if j == 0 else yy * zr
            copies.append(post(bb.at[k, j, part(at_row, zr, 8)], r2.at[k, j, n], (xs, ys)[j][n]))
        return copies

    mine_z, place = z % 2, (y * (2 * zr) + xh * zr, xh * half + y * zr)

    def third(k, arrived):
        for j in (0, 1):
            wait(arrived[j])
            at_row = xl * (2 * zr) + xh * zr if j == 0 else y * zr
            zb[k, j] = bb[k, j, part(at_row, zr, 8), :] + (r2[k, j, 0] + r2[k, j, 1] + r2[k, j, 2])
        return [post(zb.at[k, 1 - mine_z], zb.at[k, 2], z1)]

    def fourth(k, arrived):
        wait(arrived)
        cz[k, z // 2] = zb[k, mine_z] + zb[k, 2]
        here = cz.at[k, z // 2]
        return [post(here, here, zs[n]) for n in (1, 3, 5)]

    def fifth(k, arrived):
        wait(arrived)
        at_row = (1 - mine_z) * place[0] + mine_z * place[1]
        rows_, cols = part(at_row, zr, 8), part(mine_z * hc, hc, 128)
        outs[k][rows_, cols] = (cz[k, 0] + cz[k, 1]) + (cz[k, 2] + cz[k, 3])
        here = outs[k].at[rows_, cols]
        return [post(here, here, z1)]

    def sixth(k, arrived):
        wait(arrived)
        copies = []
        for j in (0, 1):
            here = outs[k].at[part(place[j], zr, 8), pl.ds(j * hc, hc)]
            copies.append([post(here, here, peer) for peer in ((x2,), ys)[j]])
        return copies

    def seventh(k, j, arrived):
        wait(arrived)
        cols = pl.ds(j * hc, hc)
        here = outs[k].at[part(y * 2 * zr, 2 * zr, 8) if j == 0 else part(xh * half, half, 8), cols]
        return [post(here, here, peer) for peer in (ys, (x2,))[j]]

    def both(stage, k, arrived):
        return [stage(k, j, arrived[j]) for j in (0, 1)]

    for q in range(4):
        here, there = pl.ds(q * fine, fine), pl.ds(rows + q * fine, fine)
        b_3[q].wait_recv()
        sz[here, :] = (d_t[there, :] + rt[there, :].astype(F32)).astype(BF)
        b_z.append(post(sz.at[here], rz.at[here], z2))
    wait(a_s)
    s1[x] = s0[0] + s0[1]
    a_s = [post(s1.at[x], s1.at[x], peer) for peer in xs]
    wait(b_i)
    a_i = back(IMG, d_i[pl.ds(0, rows), :] + ri[...].astype(F32))
    wait(a_s)
    s2[z] = (s1[0] + s1[1]) + (s1[2] + s1[3])
    a_s = [post(s2.at[z], s2.at[z], peer) for peer in zs]
    a_i = both(first, IMG, a_i)
    a_i = both(second, IMG, a_i)
    wait(a_s)
    total = s2[0]
    for n in range(1, 8):
        total = total + s2[n]
    s3[y] = total
    a_s = [post(s3.at[y], s3.at[y], peer) for peer in ys]
    wait(b_2)
    wait(b_z)
    a_t = back(TXT, d_t[pl.ds(0, rows), :] + rt[pl.ds(0, rows), :].astype(F32) + rz[...].astype(F32))
    a_i = third(IMG, a_i)
    a_t = both(first, TXT, a_t)
    a_i = fourth(IMG, a_i)
    a_t = both(second, TXT, a_t)
    a_i = fifth(IMG, a_i)
    a_t = third(TXT, a_t)
    a_i = sixth(IMG, a_i)
    a_t = fourth(TXT, a_t)
    a_i = both(seventh, IMG, a_i)
    a_t = fifth(TXT, a_t)
    a_t = sixth(TXT, a_t)
    a_t = both(seventh, TXT, a_t)
    wait(a_s)
    kinds = (s3[0] + s3[1]) + (s3[2] + s3[3])
    for n, factor in enumerate((1.0 / (images * width), 1.0 / images, 1.0 / images)):
        value = jnp.sum(jnp.sum(kinds[n], axis=1, keepdims=True), axis=0, keepdims=True) * factor
        if n == 2:
            value = value * scale[:, 0:1]
        out_s[n:n + 1, :] = jnp.broadcast_to(value, (1, 128))
    for a in a_i + a_t:
        wait(a)
    for copy in started:
        copy.wait_send()


def per_device(img_feat, txt_feat, img_proj, txt_proj, logit_scale, bias):
    rows, embed = img_feat.shape
    shard = img_proj.shape[0]
    width = rows * 8
    images = rows * lax.axis_size("batch") * lax.axis_size("mp")
    half, hc = shard // 2, embed // 2
    v = pltpu.VMEM
    scratch = [
        v((2, embed, embed), BF), v((2, embed, rows), BF),
        v((4 * rows, embed), BF), v((2 * rows, embed), BF),
        v((2, rows, embed), F32), v((2, rows, 128), F32),
        v((4 * rows, embed), F32), v((2 * rows, embed), F32),
        v((2 * rows, embed), BF), v((2 * rows, embed), BF),
        v((rows, embed), BF), v((rows, embed), BF),
        v((rows, embed), BF), v((rows, embed), BF),
        v((2, embed, embed), F32), v((2, 2, shard, embed), F32),
        v((2, 2, 3, half, hc), F32), v((2, 2, 3, half, hc), F32), v((2, 2, half, hc), F32),
        v((2, 2, 3, half // 4, hc), F32), v((2, 3, half // 4, hc), F32), v((2, 4, half // 4, hc), F32),
        v((3, 8, rows // 2), F32),
        v((2, 3, 8, 128), F32), v((4, 3, 8, 128), F32), v((8, 3, 8, 128), F32), v((4, 3, 8, 128), F32),
        pltpu.SemaphoreType.DMA((128,)), pltpu.SemaphoreType.DMA((128,)),
    ]
    vm = pl.BlockSpec(memory_space=pltpu.VMEM)
    sm = pl.BlockSpec(memory_space=pltpu.SMEM)
    g_txt, g_img, s = pl.pallas_call(
        functools.partial(kernel, (rows, embed, shard, width, images)),
        out_shape=(
            jax.ShapeDtypeStruct((shard, embed), F32),
            jax.ShapeDtypeStruct((shard, embed), F32),
            jax.ShapeDtypeStruct((8, 128), F32),
        ),
        in_specs=[sm, sm, vm, vm, vm, vm],
        out_specs=(vm, vm, vm),
        scratch_shapes=scratch,
        compiler_params=pltpu.CompilerParams(
            collective_id=0, has_side_effects=True, vmem_limit_bytes=64 * 1024 * 1024 - 65536),
    )(logit_scale.reshape(1), bias.reshape(1), img_feat, txt_feat, img_proj, txt_proj)
    return s[0, 0], s[2, 0], s[1, 0], g_img, g_txt


def solution(mesh):
    return jax.shard_map(
        per_device,
        mesh=mesh,
        in_specs=(
            P(("batch", "mp"), None),
            P(("batch", "mp"), None),
            P("mp", None),
            P("mp", None),
            P(),
            P(),
        ),
        out_specs=(P(), P(), P(), P("mp", None), P("mp", None)),
        check_vma=False,
    )
```

time: 1430 us -> 156 us (0.11)
  waiting for transfers between devices: 1250 us -> 0 us
  Pallas kernels: 0 us -> 150 us
  blocking collectives: 78.3 us -> 0 us
  matrix products: 38 us -> 0 us
  between operations: 21.2 us -> 1.94 us
  local copies, waits for them, and re-layouts: 20.8 us -> 4.11 us
    psum x1 -> x0, waiting for transfers between devices: 623 us -> none  [per_device(): summed = lax.psum(local_rows, 'batch')]
    ppermute x6 -> x0, waiting for transfers between devices: 524 us -> none  [from_partner(): lax.ppermute(value, axis, [(i, i ^ 1 << bit) for i in range(lax.axis_size...]
    pallas_call x0 -> x1, Pallas kernels: none -> 150 us  [per_device(): pl.pallas_call(functools.partial(kernel, (rows, embed, shard, width, imag...]
    psum x1 -> x0, blocking collectives: 78.3 us -> none  [per_device(): lax.psum((loss, gsum, gscale), ('batch', 'mp'))]
    unnamed x5 -> x0, waiting for transfers between devices: 55.7 us -> none
    all_gather x2 -> x0, waiting for transfers between devices: 50.6 us -> none  [the longest x1 28.2 us: per_device(): lax.all_gather(txt_proj, 'mp', axis=0, tiled=True)]
    dot_general x7 -> x0, matrix products: 38 us -> none  [the longest x1 17.4 us: pair_terms(): jnp.einsum('rd,cd->rc', left, right, preferred_element_type=jnp.float32)]
    unnamed x22 -> x4, local copies, waits for them, and re-layouts: 18.7 us -> 2.8 us
  transfers between devices with their start and end apart: 10 -> 0, of which waited for: 10 -> 0; matrix products, arithmetic and copies ran while one was open for 1% -> 0% of each run, Pallas kernels for 0% -> 0%
where the time goes in v2:
time: 156 us
  Pallas kernels  150 us (96%)
  local copies, waits for them, and re-layouts  4.11 us (3%)
  between operations  1.94 us (1%)
    pallas_call x1, Pallas kernels, per_device(): pl.pallas_call(functools.partial(kernel, (rows, embed, shard, width, imag...  150 us

profile of v2, /device:TPU:2, one launch (start us, length us, event | category | flops | bytes accessed | tf_op | source)
XLA Modules:
  0.0 155.8 jit_solution(2839347190420976661)
XLA Ops:
  1.9 149.7 %shard_map.101 = (f32[192,768]{1,0:T(8,128)}, f32[192,768]{1,0:T(8,128)}, f32[8,128]{1,0:T(8,128)}) custom-call(f32[1]{0:T(128)} %bitcast.5.ls_ref, f32[1]{0:T(128)} %bitcast.6.bias_ref, bf16[512,768]{1,0:T(8,128)(2,1)} %imgf.1, bf16[512,768]{1,0:T(8,128)(2,1)} %txtf.1, bf16[192,768]{1,0:T(8,128)(2,1)} %wi.1, bf16[192,768]{1,0:T(8,128)(2,1)} %wt.1), custom_call_target="tpu_custom_call" | custom-call | tf_op jit(solution)/shard_map/pallas_call | solution.py:378
  151.6 1.3 fusion
  153.0 0.0 copy-start
  153.0 2.0 %copy.15 = f32[192,768]{1,0:T(8,128)} copy(f32[192,768]{1,0:T(8,128)} %get-tuple-element.22) | data formatting | bytes 1179648
  154.9 0.0 copy-done
  154.9 0.8 copy.16
Async XLA Ops:
  153.0 2.0 %copy-start = (f32[192,768]{1,0:T(8,128)S(1)}, f32[192,768]{1,0:T(8,128)}, u32[]{:S(2)}) copy-start(f32[192,768]{1,0:T(8,128)} %get-tuple-element.23) | copy-start | bytes 1769476

commit v3 on v2

--- a/solution.py
+++ b/solution.py
@@ -12,12 +12,11 @@
 TXT, IMG = 0, 1
 
 
-def kernel(dims, ls_ref, bias_ref, imgf, txtf, wi, wt, out_txt, out_img, out_s,
+def kernel(dims, ls_ref, bias_ref, imgf, txtf, wi, wt, out,
            w, ft, zt, zi, zf, rr, d_t, d_i, st, rt, si, ri, sz, rz,
            p, r0, sx, rx, bb, r2, zb, cz, acc, s0, s1, s2, s3, send, recv):
     rows, embed, shard, width, images = dims
     feats = (txtf, imgf)
-    outs = (out_txt, out_img)
     b, m = lax.axis_index("batch"), lax.axis_index("mp")
     xh, z, y = b % 2, (b // 2) % 8, b // 16
     xl, c = m // 2, m % 2
@@ -71,8 +70,8 @@
         own[k] = (
             post(ws[k].at[pl.ds(0, half)], w.at[k, part(mine, half, 16)], xs[0]),
             post(ws[k].at[pl.ds(half, half)], w.at[k, part(mine + half, half, 16)], xs[2]),
-            post(ws[k], w.at[k, part(mine, shard, 16)], partner),
         )
+    own[TXT] += (post(ws[TXT], w.at[TXT, part(mine, shard, 16)], partner),)
     for k in (TXT, IMG):
         w[k, part(mine, shard, 16), :] = ws[k][...]
     scale = jnp.exp(jnp.full((1, embed), ls_ref[0], F32))
@@ -123,6 +122,7 @@
 
     passed_t = fetch(TXT)
     project(TXT, passed_t, zt, send_txt)
+    own[IMG] += (post(ws[IMG], w.at[IMG, part(mine, shard, 16)], partner),)
     passed_i = fetch(IMG)
     project(IMG, passed_i, zi, lambda here: None)
     next_img()
@@ -169,21 +169,22 @@
         lax.fori_loop(0, count, step, 0)
 
     def relay(q):
-        wait(t_z[2 * q:2 * q + 2])
-        t_d.append(post(zt.at[unit(1, q)], zt.at[unit(3, q)], x2))
+        wait(t_z[q:q + 1])
+        t_d.append(post(zt.at[small(1, q)], zt.at[small(3, q)], x2))
 
     loop(2, lambda n: tile(n * CR, CR, 0, rows, True))
     relay(0)
+    relay(1)
     wait(t_x)
+    relay(2)
     loop(2, lambda n: tile(n * CR, CR, 2 * rows, rows))
-    relay(1)
+    relay(3)
     loop(2, lambda n: tile(n * CR, CR, rows, rows))
     wait(i_z[:2])
     loop(3, lambda n: tile(rows, CR, n * rows, rows))
-    wait([t_d[0]])
+    wait(t_d[:2])
     loop(3, lambda n: tile(n * CR, CR, 3 * rows, CR))
     wait(i_z[2:])
-    tile(rows + CR, CR, 2 * rows, rows)
     b_2, b_3, b_i, b_z = [], [], [], []
 
     def send_2(q):
@@ -202,15 +203,26 @@
         si[here, :] = d_i[small(1, q), :].astype(BF)
         b_i.append(post(si.at[here], ri.at[here], z1))
 
-    send_2(0)
     tile(rows + CR, CR, 3 * rows, CR)
     send_3(0)
-    loop(2, lambda n: tile(rows + CR, CR, n * rows, rows))
-    wait([t_d[1]])
-    loop(4, lambda n: tile(n * CR, CR, 3 * rows + CR, CR))
+    loop(3, lambda n: tile(rows + CR, CR, n * rows, rows))
+
+    def pass_on(q):
+        here, there = pl.ds(q * fine, fine), pl.ds(rows + q * fine, fine)
+        b_3[q].wait_recv()
+        sz[here, :] = (d_t[there, :] + rt[there, :].astype(F32)).astype(BF)
+        b_z.append(post(sz.at[here], rz.at[here], z2))
+
+    wait(t_d[2:])
+    loop(2, lambda n: tile(n * CR, CR, 3 * rows + CR, CR))
+    pass_on(0)
+    loop(2, lambda n: tile(rows + n * CR, CR, 3 * rows + CR, CR))
     send_3(1)
+    send_2(0)
     send_2(1)
-    for q in range(4):
+    send_i(0)
+    pass_on(1)
+    for q in (1, 2, 3):
         send_i(q)
     s0[0] = acc[:, :, 0:128] + acc[:, :, 128:256]
     a_s = [post(s0.at[0], s0.at[1], partner)]
@@ -246,7 +258,7 @@
     def first(k, j, arrived):
         wait(arrived)
         copies = []
-        for n in range(3):
+        for n in (1, 0, 2):
             sx[k, j, n] = block(k, j, (y + n + 1) % 4, (x + n + 1) % 4)
             copies.append(post(sx.at[k, j, n], rx.at[k, j, n], (ys, xs)[j][n]))
         bb[k, j] = block(k, j, y, x)
@@ -256,13 +268,13 @@
         wait(arrived)
         bb[k, j] = bb[k, j] + (rx[k, j, 0] + rx[k, j, 1] + rx[k, j, 2])
         copies = []
-        for n in range(3):
+        for n in (1, 0, 2):
             xx, yy = (x + n + 1) % 4, (y + n + 1) % 4
             at_row = (xx % 2) * (2 * zr) + (xx // 2) * zr if j == 0 else yy * zr
             copies.append(post(bb.at[k, j, part(at_row, zr, 8)], r2.at[k, j, n], (xs, ys)[j][n]))
         return copies
 
-    mine_z, place = z % 2, (y * (2 * zr) + xh * zr, xh * half + y * zr)
+    mine_z = z % 2
 
     def third(k, arrived):
         for j in (0, 1):
@@ -275,38 +287,45 @@
         wait(arrived)
         cz[k, z // 2] = zb[k, mine_z] + zb[k, 2]
         here = cz.at[k, z // 2]
-        return [post(here, here, zs[n]) for n in (1, 3, 5)]
+        return [post(here, here, zs[n]) for n in (3, 1, 5)]
+
+    def chunk(k, j, yy, hi):
+        at_row = (1 - j) * (yy * (2 * zr) + hi * zr) + j * (hi * half + yy * zr)
+        return out.at[part((1 - k) * shard + at_row, zr, 8), part(j * hc, hc, 128)]
+
+    around = (ys[1], x2, ys[0], ys[2])
 
     def fifth(k, arrived):
         wait(arrived)
-        at_row = (1 - mine_z) * place[0] + mine_z * place[1]
-        rows_, cols = part(at_row, zr, 8), part(mine_z * hc, hc, 128)
-        outs[k][rows_, cols] = (cz[k, 0] + cz[k, 1]) + (cz[k, 2] + cz[k, 3])
-        here = outs[k].at[rows_, cols]
-        return [post(here, here, z1)]
+        here = chunk(k, mine_z, y, xh)
+        here[...] = (cz[k, 0] + cz[k, 1]) + (cz[k, 2] + cz[k, 3])
+        return [post(here, here, z1)], [post(here, here, peer) for peer in around]
 
     def sixth(k, arrived):
+        wait(arrived[0])
+        here = chunk(k, 1 - mine_z, y, xh)
+        return arrived[1], [post(here, here, peer) for peer in around]
+
+    def spread(k, j, arrived):
         wait(arrived)
         copies = []
-        for j in (0, 1):
-            here = outs[k].at[part(place[j], zr, 8), pl.ds(j * hc, hc)]
-            copies.append([post(here, here, peer) for peer in ((x2,), ys)[j]])
+        for n in (1, 0, 2):
+            here = chunk(k, j, (y + j * (n + 1)) % 4, (xh + 1 - j) % 2)
+            peer = tuple((1 - j) * a + j * d for a, d in zip(ys[n], x2))
+            copies.append(post(here, here, peer))
         return copies
 
-    def seventh(k, j, arrived):
-        wait(arrived)
-        cols = pl.ds(j * hc, hc)
-        here = outs[k].at[part(y * 2 * zr, 2 * zr, 8) if j == 0 else part(xh * half, half, 8), cols]
-        return [post(here, here, peer) for peer in (ys, (x2,))[j]]
+    def seventh(k, arrived):
+        return spread(k, mine_z, arrived[0]), arrived[1]
+
+    def eighth(k, arrived):
+        return [arrived[0], spread(k, 1 - mine_z, arrived[1])]
 
     def both(stage, k, arrived):
         return [stage(k, j, arrived[j]) for j in (0, 1)]
 
-    for q in range(4):
-        here, there = pl.ds(q * fine, fine), pl.ds(rows + q * fine, fine)
-        b_3[q].wait_recv()
-        sz[here, :] = (d_t[there, :] + rt[there, :].astype(F32)).astype(BF)
-        b_z.append(post(sz.at[here], rz.at[here], z2))
+    pass_on(2)
+    pass_on(3)
     wait(a_s)
     s1[x] = s0[0] + s0[1]
     a_s = [post(s1.at[x], s1.at[x], peer) for peer in xs]
@@ -334,17 +353,19 @@
     a_t = third(TXT, a_t)
     a_i = sixth(IMG, a_i)
     a_t = fourth(TXT, a_t)
-    a_i = both(seventh, IMG, a_i)
+    a_i = seventh(IMG, a_i)
+    a_i = eighth(IMG, a_i)
     a_t = fifth(TXT, a_t)
     a_t = sixth(TXT, a_t)
-    a_t = both(seventh, TXT, a_t)
+    a_t = seventh(TXT, a_t)
+    a_t = eighth(TXT, a_t)
     wait(a_s)
     kinds = (s3[0] + s3[1]) + (s3[2] + s3[3])
     for n, factor in enumerate((1.0 / (images * width), 1.0 / images, 1.0 / images)):
         value = jnp.sum(jnp.sum(kinds[n], axis=1, keepdims=True), axis=0, keepdims=True) * factor
         if n == 2:
             value = value * scale[:, 0:1]
-        out_s[n:n + 1, :] = jnp.broadcast_to(value, (1, 128))
+        out[2 * shard + n:2 * shard + n + 1, 0:128] = jnp.broadcast_to(value, (1, 128))
     for a in a_i + a_t:
         wait(a)
     for copy in started:
@@ -375,20 +396,17 @@
     ]
     vm = pl.BlockSpec(memory_space=pltpu.VMEM)
     sm = pl.BlockSpec(memory_space=pltpu.SMEM)
-    g_txt, g_img, s = pl.pallas_call(
+    g = pl.pallas_call(
         functools.partial(kernel, (rows, embed, shard, width, images)),
-        out_shape=(
-            jax.ShapeDtypeStruct((shard, embed), F32),
-            jax.ShapeDtypeStruct((shard, embed), F32),
-            jax.ShapeDtypeStruct((8, 128), F32),
-        ),
+        out_shape=jax.ShapeDtypeStruct((2 * shard + 8, embed), F32),
         in_specs=[sm, sm, vm, vm, vm, vm],
-        out_specs=(vm, vm, vm),
+        out_specs=vm,
         scratch_shapes=scratch,
         compiler_params=pltpu.CompilerParams(
             collective_id=0, has_side_effects=True, vmem_limit_bytes=64 * 1024 * 1024 - 65536),
     )(logit_scale.reshape(1), bias.reshape(1), img_feat, txt_feat, img_proj, txt_proj)
-    return s[0, 0], s[2, 0], s[1, 0], g_img, g_txt
+    s = g[2 * shard:]
+    return s[0, 0], s[2, 0], s[1, 0], g[:shard], g[shard:2 * shard]
 
 
 def solution(mesh):

time: 156 us -> 155 us (level)
    unnamed x4 -> x0, local copies, waits for them, and re-layouts: 2.8 us -> none
    slice x1 -> x2, local copies, waits for them, and re-layouts: 1.31 us -> 3.63 us  [per_device(): return (s[0, 0], s[2, 0], s[1, 0], g[:shard], g[shard:2 * shard])]
where the time goes in v3:
time: 155 us
  Pallas kernels  150 us (97%)
  local copies, waits for them, and re-layouts  3.63 us (2%)
  between operations  1.93 us (1%)
    pallas_call x1, Pallas kernels, per_device(): pl.pallas_call(functools.partial(kernel, (rows, embed, shard, width, imag...  150 us
    slice x2, local copies, waits for them, and re-layouts, per_device(): return (s[0, 0], s[2, 0], s[1, 0], g[:shard], g[shard:2 * shard])  3.63 us

profile of v3, /device:TPU:2, one launch (start us, length us, event | category | flops | bytes accessed | tf_op | source)
XLA Modules:
  0.0 155.2 jit_solution(6409618137752364490)
XLA Ops:
  1.9 149.7 %shard_map.101 = f32[392,768]{1,0:T(8,128)} custom-call(f32[1]{0:T(128)} %bitcast.5.ls_ref, f32[1]{0:T(128)} %bitcast.6.bias_ref, bf16[512,768]{1,0:T(8,128)(2,1)} %imgf.1, bf16[512,768]{1,0:T(8,128)(2,1)} %txtf.1, bf16[192,768]{1,0:T(8,128)(2,1)} %wi.1, bf16[192,768]{1,0:T(8,128)(2,1)} %wt.1), custom_call_target="tpu_custom_call" | custom-call | tf_op jit(solution)/shard_map/pallas_call | solution.py:399
  151.6 1.3 fusion.1
  152.9 2.3 %fusion = (f32[192,768]{1,0:T(8,128)}, f32[192,768]{1,0:T(8,128)}) fusion(f32[392,768]{1,0:T(8,128)} %shard_map.101), kind=kLoop, calls=%fused_computation | loop fusion | bytes 2359296 | tf_op jit(solution)/shard_map/slice | solution.py:409

commit v4 on v3

--- a/solution.py
+++ b/solution.py
@@ -335,7 +335,6 @@
     s2[z] = (s1[0] + s1[1]) + (s1[2] + s1[3])
     a_s = [post(s2.at[z], s2.at[z], peer) for peer in zs]
     a_i = both(first, IMG, a_i)
-    a_i = both(second, IMG, a_i)
     wait(a_s)
     total = s2[0]
     for n in range(1, 8):
@@ -345,8 +344,9 @@
     wait(b_2)
     wait(b_z)
     a_t = back(TXT, d_t[pl.ds(0, rows), :] + rt[pl.ds(0, rows), :].astype(F32) + rz[...].astype(F32))
+    a_i = both(second, IMG, a_i)
+    a_t = both(first, TXT, a_t)
     a_i = third(IMG, a_i)
-    a_t = both(first, TXT, a_t)
     a_i = fourth(IMG, a_i)
     a_t = both(second, TXT, a_t)
     a_i = fifth(IMG, a_i)

time: 155 us -> 156 us (level)
  no operation moved by 1% of the time
where the time goes in v4:
time: 156 us; the launch traced here: 155 us
  Pallas kernels  149 us (96%)
  local copies, waits for them, and re-layouts  3.63 us (2%)
  between operations  1.93 us (1%)
    pallas_call x1, Pallas kernels, per_device(): pl.pallas_call(functools.partial(kernel, (rows, embed, shard, width, imag...  149 us
    slice x2, local copies, waits for them, and re-layouts, per_device(): return (s[0, 0], s[2, 0], s[1, 0], g[:shard], g[shard:2 * shard])  3.63 us

profile of v4, /device:TPU:2, one launch (start us, length us, event | category | flops | bytes accessed | tf_op | source)
XLA Modules:
  0.0 155.1 jit_solution(10412595156289230009)
XLA Ops:
  1.9 149.5 %shard_map.101 = f32[392,768]{1,0:T(8,128)} custom-call(f32[1]{0:T(128)} %bitcast.5.ls_ref, f32[1]{0:T(128)} %bitcast.6.bias_ref, bf16[512,768]{1,0:T(8,128)(2,1)} %imgf.1, bf16[512,768]{1,0:T(8,128)(2,1)} %txtf.1, bf16[192,768]{1,0:T(8,128)(2,1)} %wi.1, bf16[192,768]{1,0:T(8,128)(2,1)} %wt.1), custom_call_target="tpu_custom_call" | custom-call | tf_op jit(solution)/shard_map/pallas_call | solution.py:399
  151.4 1.3 fusion.1
  152.7 2.3 %fusion = (f32[192,768]{1,0:T(8,128)}, f32[192,768]{1,0:T(8,128)}) fusion(f32[392,768]{1,0:T(8,128)} %shard_map.101), kind=kLoop, calls=%fused_computation | loop fusion | bytes 2359296 | tf_op jit(solution)/shard_map/slice | solution.py:409
